TPU v7x, 512 devices: a whole 4x8x8 slice. The times are simulated.
512 devices in a mesh: seq: 32 (over x, z), exp: 16 (over y, core).
Axes of the slice: x: 4, y: 8, z: 8, core: 2. Of those that a mesh axis runs over, the one named last changes fastest.
Arguments:
- queries: bfloat16 [8192, 2048], P('seq', 'exp'), may hold values from -112 to 112
- key_rows: bfloat16 [8192, 2048], P('seq', 'exp'), may hold values from -4 to 4
- value_rows: bfloat16 [8192, 2048], P('seq', 'exp'), may hold values from -6 to 6
- out_grad: bfloat16 [8192, 2048], P('seq', 'exp'), may hold values from -6 to 6
- expert_ids: int32 [8192, 2], P('seq'), may hold values from 0 to 31, all different within a row
- gate_values: float32 [8192, 2], P('seq'), may hold values from 0.1 to 1
- alibi_slope: float32 [16], P('exp'), may hold values from 0.00012207031 to 0.1
- expert_in: bfloat16 [32, 2048, 4096], P('seq', None, 'exp'), may hold values from -0.125 to 0.125
- expert_out: bfloat16 [32, 4096, 2048], P('seq', 'exp'), may hold values from -0.09375 to 0.09375
Outputs:
- query_grad: bfloat16 [8192, 2048], P('seq', 'exp')
- key_grad: bfloat16 [8192, 2048], P('seq', 'exp')
- value_grad: bfloat16 [8192, 2048], P('seq', 'exp')
- expert_in_grad: bfloat16 [32, 2048, 4096], P('seq', None, 'exp')
- expert_out_grad: bfloat16 [32, 4096, 2048], P('seq', 'exp')
Inputs may be any that keep to these rules, and one draw needn't show every extreme that they name: `expert_ids`: each token names two different experts.
All inputs are finite; a program needn't handle non-finite values.
Results may differ from a plain program's by a relative error of at most 0.024.
Values may be sent and summed in bfloat16 or wider, within the bound.
A program may use at most 128 MiB of HBM per device.

v0:
```python
import jax
import jax.numpy as jnp
from jax import lax
from jax.sharding import PartitionSpec as P

HD = 128
WCH = 16


def shifted(block, axis, distance):
    devices = range(lax.axis_size(axis))
    route = [(i - distance, i) for i in devices if i - distance in devices]
    return lax.ppermute(block, axis, route)


def window_scores(query_heads, key_stack, slopes, seq_index, window):
    score_scale = HD ** (-0.5)
    block_len = query_heads.shape[0]
    raw_scores = (
        jnp.einsum("ihd,jhd->hij", query_heads, key_stack, preferred_element_type=jnp.float32)
        * score_scale
    )
    row_pos = lax.broadcasted_iota(jnp.int32, (block_len, key_stack.shape[0]), 0)
    col_pos = lax.broadcasted_iota(jnp.int32, (block_len, key_stack.shape[0]), 1)
    back_block = col_pos // block_len
    distance = row_pos - col_pos % block_len + back_block * block_len
    in_window = (distance >= 0) & (distance < window) & (seq_index - back_block >= 0)
    biased = raw_scores - slopes[:, None, None] * distance.astype(jnp.float32)[None]
    return jnp.where(in_window[None], biased, -jnp.inf)


def slot_routing(expert_ids, experts, capacity):
    flat_ids = jnp.concatenate([expert_ids[:, 0], expert_ids[:, 1]])
    entry_count = flat_ids.shape[0]
    expert_cols = lax.broadcasted_iota(jnp.int32, (entry_count, experts), 1)
    one_hot = (flat_ids[:, None] == expert_cols).astype(jnp.int32)
    before = jnp.cumsum(one_hot, axis=0) - one_hot
    position = jnp.sum(before * one_hot, axis=1)
    is_kept = position < capacity
    slot_index = flat_ids * capacity + position
    slot_rows = lax.broadcasted_iota(jnp.int32, (experts * capacity, entry_count), 0)
    return ((slot_rows == slot_index[None, :]) & is_kept[None, :]).astype(jnp.bfloat16)


def per_device(
    queries,
    key_rows,
    value_rows,
    out_grad,
    expert_ids,
    gate_values,
    alibi_slope,
    expert_in,
    expert_out,
):
    score_scale = HD ** (-0.5)
    block_len = queries.shape[0]
    features = queries.shape[1]
    head_count = features // HD
    seq_index = lax.axis_index("seq")
    stretches = WCH + 1
    window = WCH * block_len

    def relay_keys(step, carry):
        stack_keys, stack_values, current_keys, current_values = carry
        current_keys, current_values = shifted((current_keys, current_values), "seq", 1)
        stack_keys = lax.dynamic_update_index_in_dim(stack_keys, current_keys, step, 0)
        stack_values = lax.dynamic_update_index_in_dim(stack_values, current_values, step, 0)
        return (stack_keys, stack_values, current_keys, current_values)

    empty_stack = jnp.zeros((stretches, block_len, features), jnp.bfloat16)
    start_keys = lax.dynamic_update_index_in_dim(empty_stack, key_rows, 0, 0)
    start_values = lax.dynamic_update_index_in_dim(empty_stack, value_rows, 0, 0)
    key_stack, value_stack, unused_keys, unused_values = lax.fori_loop(
        1, stretches, relay_keys, (start_keys, start_values, key_rows, value_rows)
    )
    key_block = key_stack.reshape(stretches * block_len, head_count, HD)
    value_block = value_stack.reshape(stretches * block_len, head_count, HD)
    query_heads = queries.reshape(block_len, head_count, HD)
    scores = window_scores(query_heads, key_block, alibi_slope, seq_index, window)
    log_norm = jax.nn.logsumexp(scores, axis=2)
    probs_full = jnp.exp(scores - log_norm[:, :, None])
    weights = probs_full.astype(jnp.bfloat16)
    attn_heads = jnp.einsum(
        "hij,jhd->ihd", weights, value_block, preferred_element_type=jnp.float32
    ).astype(jnp.bfloat16)
    attn_out = attn_heads.reshape(block_len, features)
    experts = lax.axis_size("seq")
    capacity = 5 * block_len // (2 * experts)
    routing = slot_routing(expert_ids, experts, capacity)
    both_tokens = jnp.concatenate([attn_out, attn_out])
    scaled_grad = jnp.concatenate(
        [gate_values[:, 0:1] * out_grad, gate_values[:, 1:2] * out_grad]
    ).astype(jnp.bfloat16)
    send_tokens = jnp.dot(routing, both_tokens, preferred_element_type=jnp.float32).astype(
        jnp.bfloat16
    )
    send_grads = jnp.dot(routing, scaled_grad, preferred_element_type=jnp.float32).astype(
        jnp.bfloat16
    )
    recv_tokens, recv_grads = (
        lax.all_to_all(send_tokens, "seq", split_axis=0, concat_axis=0, tiled=True),
        lax.all_to_all(send_grads, "seq", split_axis=0, concat_axis=0, tiled=True),
    )
    weight_in = expert_in[0]
    weight_out = expert_out[0]
    full_tokens = lax.all_gather(recv_tokens, "exp", axis=1, tiled=True)
    pre_act = jnp.dot(full_tokens, weight_in, preferred_element_type=jnp.float32)
    full_grads = lax.all_gather(recv_grads, "exp", axis=1, tiled=True)
    logistic = jax.nn.sigmoid(pre_act)
    hidden = (pre_act * logistic).astype(jnp.bfloat16)
    through_out = lax.dot_general(
        full_grads, weight_out, (((1,), (1,)), ((), ())), preferred_element_type=jnp.float32
    )
    hidden_grad = (through_out * logistic * (1.0 + pre_act * (1.0 - logistic))).astype(jnp.bfloat16)
    out_weight_grad = lax.dot_general(
        hidden, full_grads, (((0,), (0,)), ((), ())), preferred_element_type=jnp.float32
    ).astype(jnp.bfloat16)
    in_weight_grad = lax.dot_general(
        full_tokens, hidden_grad, (((0,), (0,)), ((), ())), preferred_element_type=jnp.float32
    ).astype(jnp.bfloat16)
    back_rows = lax.psum_scatter(
        lax.dot_general(
            weight_in, hidden_grad, (((1,), (1,)), ((), ())), preferred_element_type=jnp.float32
        ).astype(jnp.bfloat16),
        "exp",
        scatter_dimension=0,
        tiled=True,
    )
    returned = lax.all_to_all(back_rows, "seq", split_axis=1, concat_axis=1, tiled=True)
    combined = lax.dot_general(
        routing, returned, (((0,), (1,)), ((), ())), preferred_element_type=jnp.float32
    )
    attn_grad = (out_grad.astype(jnp.float32) + combined[:block_len] + combined[block_len:]).astype(
        jnp.bfloat16
    )
    grad_heads = attn_grad.reshape(block_len, head_count, HD)
    row_delta = jnp.einsum(
        "ihd,ihd->hi", grad_heads, attn_heads, preferred_element_type=jnp.float32
    )
    dprob = jnp.einsum("ihd,jhd->hij", grad_heads, value_block, preferred_element_type=jnp.float32)
    dscore = (probs_full * (dprob - row_delta[:, :, None])).astype(jnp.bfloat16)
    query_grad = (
        jnp.einsum("hij,jhd->ihd", dscore, key_block, preferred_element_type=jnp.float32)
        * score_scale
    ).astype(jnp.bfloat16)
    key_parts = (
        jnp.einsum("hij,ihd->jhd", dscore, query_heads, preferred_element_type=jnp.float32)
        * score_scale
    ).reshape(stretches, block_len, features)
    value_parts = jnp.einsum(
        "hij,ihd->jhd", weights, grad_heads, preferred_element_type=jnp.float32
    ).reshape(stretches, block_len, features)

    def relay_grads(step, carry):
        key_acc, value_acc = carry
        key_acc, value_acc = (
            shifted(key_acc.astype(jnp.bfloat16), "seq", -1).astype(key_acc.dtype),
            shifted(value_acc.astype(jnp.bfloat16), "seq", -1).astype(value_acc.dtype),
        )
        index = stretches - 1 - step
        key_acc = key_acc + lax.dynamic_index_in_dim(key_parts, index, 0, keepdims=False)
        value_acc = value_acc + lax.dynamic_index_in_dim(value_parts, index, 0, keepdims=False)
        return (key_acc, value_acc)

    key_total, value_total = lax.fori_loop(
        1, stretches, relay_grads, (key_parts[stretches - 1], value_parts[stretches - 1])
    )
    key_grad = key_total.astype(jnp.bfloat16)
    value_grad = value_total.astype(jnp.bfloat16)
    return (
        query_grad.reshape(block_len, features),
        key_grad,
        value_grad,
        in_weight_grad[None],
        out_weight_grad[None],
    )


def solution(mesh):
    return jax.shard_map(
        per_device,
        mesh=mesh,
        in_specs=(
            P("seq", "exp"),
            P("seq", "exp"),
            P("seq", "exp"),
            P("seq", "exp"),
            P("seq", None),
            P("seq", None),
            P("exp"),
            P("seq", None, "exp"),
            P("seq", "exp", None),
        ),
        out_specs=(
            P("seq", "exp"),
            P("seq", "exp"),
            P("seq", "exp"),
            P("seq", None, "exp"),
            P("seq", "exp", None),
        ),
        check_vma=False,
    )
```

profile of v0, /device:TPU:2, one launch (start us, length us, event | category | flops | bytes accessed | tf_op | source)
XLA Modules:
  0.0 586.6 jit_solution(2084339012505833438)
XLA Ops:
  14.8 170.1 %while.36 = (s32[]{:T(128)}, bf16[17,256,128]{2,1,0:T(8,128)(2,1)S(1)}, bf16[17,256,128]{2,1,0:T(8,128)(2,1)S(1)}, bf16[256,128]{1,0:T(8,128)(2,1)S(1)}, bf16[25...) while((s32[]{:T(128)}, bf16[17,256,128]{2,1,0:T(8,128)(2,1)S(1)}, ...), condition=%wide.region_1.2_spmd, body=%wide.region_0.1_spmd.sunk | while | flops 5 | bytes 1048783 | solution.py:74
  14.8 4.3 collective-permute-start.1
  19.1 4.3 collective-permute-start
  23.4 4.6 collective-permute-done.1
  35.1 3.7 collective-permute-done.1
  42.1 3.8 collective-permute-start
  52.4 4.0 collective-permute-start
  62.6 3.7 collective-permute-start
  85.1 4.4 collective-permute-done.1
  95.3 4.4 collective-permute-done.1
  106.2 5.0 collective-permute-done.1
  117.0 4.4 collective-permute-done.1
  127.3 5.0 collective-permute-done.1
  137.5 4.8 collective-permute-done.1
  147.8 4.4 collective-permute-done.1
  158.0 4.4 collective-permute-done.1
  168.3 4.4 collective-permute-done.1
  178.5 4.4 collective-permute-done.1
  184.9 5.8 fusion.71
  194.7 15.8 %all_to_all.36 = bf16[32,20,128]{2,1,0:T(8,128)(2,1)} all-to-all(bf16[32,20,128]{2,1,0:T(8,128)(2,1)S(1)} %all_to_all.27), channel_id=1, replica_groups=mesh['seq'=32,'exp'=16] {'seq'}, dimensions={0} | all-to-all | bytes 327680 | tf_op jit(solution)/shard_map/all_to_all | solution.py:102
  215.3 15.9 %all_to_all.37 = bf16[32,20,128]{2,1,0:T(8,128)(2,1)} all-to-all(bf16[32,20,128]{2,1,0:T(8,128)(2,1)S(1)} %all_to_all.24), channel_id=1, replica_groups=mesh['seq'=32,'exp'=16] {'seq'}, dimensions={0} | all-to-all | bytes 327680 | tf_op jit(solution)/shard_map/all_to_all | solution.py:103
  232.9 22.8 %all-gather.5.cloned.1.call-done = bf16[640,2048]{1,0:T(8,128)(2,1)} async-done(((bf16[640,128]{1,0:T(8,128)(2,1)}), bf16[640,2048]{1,0:T(8,128)(2,1)}) %all-gather.5.cloned.1.call-update) | async-done | bytes 2621456 | tf_op jit(solution)/shard_map/all_gather | solution.py:107
  259.2 43.8 %all-gather.3.cloned.1.call-done = bf16[640,2048]{1,0:T(8,128)(2,1)} async-done(((bf16[640,128]{1,0:T(8,128)(2,1)}), bf16[640,2048]{1,0:T(8,128)(2,1)}) %all-gather.3.cloned.1.call-update) | async-done | bytes 2621456 | tf_op jit(solution)/shard_map/all_gather | solution.py:109
  309.2 4.4 copy.33
  313.6 4.0 fusion.14
  317.6 57.7 %reduce-scatter.4.cloned.1.call-done = bf16[128,640]{1,0:T(8,128)(2,1)} async-done(((bf16[2048,640]{1,0:T(8,128)(2,1)}), bf16[128,640]{1,0:T(8,128)(2,1)}) %reduce-scatter.4.cloned.1.call-update) | async-done | bytes 163856
  377.0 10.5 %all-to-all-start.2 = ((bf16[128,32,20]{0,2,1:T(8,128)(2,1)}), bf16[128,32,20]{0,2,1:T(8,128)(2,1)S(1)}, u32[]{:S(2)}, u32[]{:S(2)}) async-start(bf16[128,32,20]{0,2,1:T(8,128)(2,1)} %all_to_all.30), calls=%async_computation.2 | async-start | bytes 393216 | tf_op jit(solution)/shard_map/all_to_all | solution.py:130
  387.5 3.8 fusion.13
  391.3 5.7 all-to-all-done.2
  403.4 4.0 fusion.4
  412.9 166.5 %while.37 = (s32[]{:T(128)}, bf16[256,128]{1,0:T(8,128)(2,1)S(1)}, bf16[256,128]{1,0:T(8,128)(2,1)S(1)}, f32[17,256,128]{2,1,0:T(8,128)S(1)}, f32[17,256,128]{2,...) while((s32[]{:T(128)}, bf16[256,128]{1,0:T(8,128)(2,1)S(1)}, ...), condition=%wide.region_9.10_spmd, body=%wide.region_8.9_spmd.sunk | while | flops 196614 | bytes 1048803 | solution.py:166
  416.1 3.6 collective-permute-start.2
  422.3 5.7 collective-permute-start.3
  434.2 4.2 collective-permute-start.3
  444.6 4.0 collective-permute-start.3
  455.3 4.2 collective-permute-start.3
  465.7 4.0 collective-permute-start.3
  475.9 4.0 collective-permute-start.3
  486.2 4.0 collective-permute-start.3
  496.4 4.0 collective-permute-start.3
  506.6 4.0 collective-permute-start.3
  513.7 3.6 collective-permute-done.2
  517.3 3.6 collective-permute-start.3
  527.1 4.0 collective-permute-start.3
  537.3 4.6 collective-permute-start.3
  548.6 4.2 collective-permute-start.3
  559.0 4.0 collective-permute-start.3
  569.2 4.0 collective-permute-start.3
  (264 shorter events, 232.5 us)
Async XLA Ops:
  7.2 248.6 %all-gather.5.cloned.1.call-start = ((), (), s32[]{:S(2)}) async-start(), calls=%async_computation.5 | async-start | bytes 2785280 | tf_op jit(solution)/shard_map/all_gather | solution.py:107
  14.8 13.2 %collective-permute-start.1 = (bf16[256,128]{1,0:T(8,128)(2,1)S(1)}, bf16[256,128]{1,0:T(8,128)(2,1)S(1)}, u32[]{:S(2)}, u32[]{:S(2)}) collective-permute-start(bf16[256,128]{1,0:T(8,128)(2,1)S(1)} %get-tuple-element.375), channel_id=1, source_target_pairs={{0,16},{16,32},{32,48},{48,64},{64,80},{80,96},{96,112},{112,128},... | collective-permute-start | bytes 196616 | tf_op jit(solution)/shard_map/while/body/eval_jaxpr/ppermute | solution.py:13
  19.1 10.8 %collective-permute-start = (bf16[256,128]{1,0:T(8,128)(2,1)S(1)}, bf16[256,128]{1,0:T(8,128)(2,1)S(1)}, u32[]{:S(2)}, u32[]{:S(2)}) collective-permute-start(bf16[256,128]{1,0:T(8,128)(2,1)S(1)} %get-tuple-element.374), channel_id=1, source_target_pairs={{0,16},{16,32},{32,48},{48,64},{64,80},{80,96},{96,112},{112,128},... | collective-permute-start | bytes 196616 | tf_op jit(solution)/shard_map/while/body/eval_jaxpr/ppermute | solution.py:13
  30.0 8.9 %collective-permute-start.1 = (bf16[256,128]{1,0:T(8,128)(2,1)S(1)}, bf16[256,128]{1,0:T(8,128)(2,1)S(1)}, u32[]{:S(2)}, u32[]{:S(2)}) collective-permute-start(bf16[256,128]{1,0:T(8,128)(2,1)S(1)} %get-tuple-element.375), channel_id=1, source_target_pairs={{0,16},{16,32},{32,48},{48,64},{64,80},{80,96},{96,112},{112,128},... | collective-permute-start | bytes 196616 | tf_op jit(solution)/shard_map/while/body/eval_jaxpr/ppermute | solution.py:13
  31.9 8.3 %collective-permute-start = (bf16[256,128]{1,0:T(8,128)(2,1)S(1)}, bf16[256,128]{1,0:T(8,128)(2,1)S(1)}, u32[]{:S(2)}, u32[]{:S(2)}) collective-permute-start(bf16[256,128]{1,0:T(8,128)(2,1)S(1)} %get-tuple-element.374), channel_id=1, source_target_pairs={{0,16},{16,32},{32,48},{48,64},{64,80},{80,96},{96,112},{112,128},... | collective-permute-start | bytes 196616 | tf_op jit(solution)/shard_map/while/body/eval_jaxpr/ppermute | solution.py:13
  40.2 8.7 %collective-permute-start.1 = (bf16[256,128]{1,0:T(8,128)(2,1)S(1)}, bf16[256,128]{1,0:T(8,128)(2,1)S(1)}, u32[]{:S(2)}, u32[]{:S(2)}) collective-permute-start(bf16[256,128]{1,0:T(8,128)(2,1)S(1)} %get-tuple-element.375), channel_id=1, source_target_pairs={{0,16},{16,32},{32,48},{48,64},{64,80},{80,96},{96,112},{112,128},... | collective-permute-start | bytes 196616 | tf_op jit(solution)/shard_map/while/body/eval_jaxpr/ppermute | solution.py:13
  42.1 8.3 %collective-permute-start = (bf16[256,128]{1,0:T(8,128)(2,1)S(1)}, bf16[256,128]{1,0:T(8,128)(2,1)S(1)}, u32[]{:S(2)}, u32[]{:S(2)}) collective-permute-start(bf16[256,128]{1,0:T(8,128)(2,1)S(1)} %get-tuple-element.374), channel_id=1, source_target_pairs={{0,16},{16,32},{32,48},{48,64},{64,80},{80,96},{96,112},{112,128},... | collective-permute-start | bytes 196616 | tf_op jit(solution)/shard_map/while/body/eval_jaxpr/ppermute | solution.py:13
  50.5 8.3 %collective-permute-start.1 = (bf16[256,128]{1,0:T(8,128)(2,1)S(1)}, bf16[256,128]{1,0:T(8,128)(2,1)S(1)}, u32[]{:S(2)}, u32[]{:S(2)}) collective-permute-start(bf16[256,128]{1,0:T(8,128)(2,1)S(1)} %get-tuple-element.375), channel_id=1, source_target_pairs={{0,16},{16,32},{32,48},{48,64},{64,80},{80,96},{96,112},{112,128},... | collective-permute-start | bytes 196616 | tf_op jit(solution)/shard_map/while/body/eval_jaxpr/ppermute | solution.py:13
  52.4 8.3 %collective-permute-start = (bf16[256,128]{1,0:T(8,128)(2,1)S(1)}, bf16[256,128]{1,0:T(8,128)(2,1)S(1)}, u32[]{:S(2)}, u32[]{:S(2)}) collective-permute-start(bf16[256,128]{1,0:T(8,128)(2,1)S(1)} %get-tuple-element.374), channel_id=1, source_target_pairs={{0,16},{16,32},{32,48},{48,64},{64,80},{80,96},{96,112},{112,128},... | collective-permute-start | bytes 196616 | tf_op jit(solution)/shard_map/while/body/eval_jaxpr/ppermute | solution.py:13
  60.7 8.3 %collective-permute-start.1 = (bf16[256,128]{1,0:T(8,128)(2,1)S(1)}, bf16[256,128]{1,0:T(8,128)(2,1)S(1)}, u32[]{:S(2)}, u32[]{:S(2)}) collective-permute-start(bf16[256,128]{1,0:T(8,128)(2,1)S(1)} %get-tuple-element.375), channel_id=1, source_target_pairs={{0,16},{16,32},{32,48},{48,64},{64,80},{80,96},{96,112},{112,128},... | collective-permute-start | bytes 196616 | tf_op jit(solution)/shard_map/while/body/eval_jaxpr/ppermute | solution.py:13
  62.6 8.3 %collective-permute-start = (bf16[256,128]{1,0:T(8,128)(2,1)S(1)}, bf16[256,128]{1,0:T(8,128)(2,1)S(1)}, u32[]{:S(2)}, u32[]{:S(2)}) collective-permute-start(bf16[256,128]{1,0:T(8,128)(2,1)S(1)} %get-tuple-element.374), channel_id=1, source_target_pairs={{0,16},{16,32},{32,48},{48,64},{64,80},{80,96},{96,112},{112,128},... | collective-permute-start | bytes 196616 | tf_op jit(solution)/shard_map/while/body/eval_jaxpr/ppermute | solution.py:13
  71.0 8.3 %collective-permute-start.1 = (bf16[256,128]{1,0:T(8,128)(2,1)S(1)}, bf16[256,128]{1,0:T(8,128)(2,1)S(1)}, u32[]{:S(2)}, u32[]{:S(2)}) collective-permute-start(bf16[256,128]{1,0:T(8,128)(2,1)S(1)} %get-tuple-element.375), channel_id=1, source_target_pairs={{0,16},{16,32},{32,48},{48,64},{64,80},{80,96},{96,112},{112,128},... | collective-permute-start | bytes 196616 | tf_op jit(solution)/shard_map/while/body/eval_jaxpr/ppermute | solution.py:13
  72.9 8.3 %collective-permute-start = (bf16[256,128]{1,0:T(8,128)(2,1)S(1)}, bf16[256,128]{1,0:T(8,128)(2,1)S(1)}, u32[]{:S(2)}, u32[]{:S(2)}) collective-permute-start(bf16[256,128]{1,0:T(8,128)(2,1)S(1)} %get-tuple-element.374), channel_id=1, source_target_pairs={{0,16},{16,32},{32,48},{48,64},{64,80},{80,96},{96,112},{112,128},... | collective-permute-start | bytes 196616 | tf_op jit(solution)/shard_map/while/body/eval_jaxpr/ppermute | solution.py:13
  81.2 8.3 %collective-permute-start.1 = (bf16[256,128]{1,0:T(8,128)(2,1)S(1)}, bf16[256,128]{1,0:T(8,128)(2,1)S(1)}, u32[]{:S(2)}, u32[]{:S(2)}) collective-permute-start(bf16[256,128]{1,0:T(8,128)(2,1)S(1)} %get-tuple-element.375), channel_id=1, source_target_pairs={{0,16},{16,32},{32,48},{48,64},{64,80},{80,96},{96,112},{112,128},... | collective-permute-start | bytes 196616 | tf_op jit(solution)/shard_map/while/body/eval_jaxpr/ppermute | solution.py:13
  83.1 8.3 %collective-permute-start = (bf16[256,128]{1,0:T(8,128)(2,1)S(1)}, bf16[256,128]{1,0:T(8,128)(2,1)S(1)}, u32[]{:S(2)}, u32[]{:S(2)}) collective-permute-start(bf16[256,128]{1,0:T(8,128)(2,1)S(1)} %get-tuple-element.374), channel_id=1, source_target_pairs={{0,16},{16,32},{32,48},{48,64},{64,80},{80,96},{96,112},{112,128},... | collective-permute-start | bytes 196616 | tf_op jit(solution)/shard_map/while/body/eval_jaxpr/ppermute | solution.py:13
  91.5 8.3 %collective-permute-start.1 = (bf16[256,128]{1,0:T(8,128)(2,1)S(1)}, bf16[256,128]{1,0:T(8,128)(2,1)S(1)}, u32[]{:S(2)}, u32[]{:S(2)}) collective-permute-start(bf16[256,128]{1,0:T(8,128)(2,1)S(1)} %get-tuple-element.375), channel_id=1, source_target_pairs={{0,16},{16,32},{32,48},{48,64},{64,80},{80,96},{96,112},{112,128},... | collective-permute-start | bytes 196616 | tf_op jit(solution)/shard_map/while/body/eval_jaxpr/ppermute | solution.py:13
  93.4 8.9 %collective-permute-start = (bf16[256,128]{1,0:T(8,128)(2,1)S(1)}, bf16[256,128]{1,0:T(8,128)(2,1)S(1)}, u32[]{:S(2)}, u32[]{:S(2)}) collective-permute-start(bf16[256,128]{1,0:T(8,128)(2,1)S(1)} %get-tuple-element.374), channel_id=1, source_target_pairs={{0,16},{16,32},{32,48},{48,64},{64,80},{80,96},{96,112},{112,128},... | collective-permute-start | bytes 196616 | tf_op jit(solution)/shard_map/while/body/eval_jaxpr/ppermute | solution.py:13
  102.3 8.9 %collective-permute-start.1 = (bf16[256,128]{1,0:T(8,128)(2,1)S(1)}, bf16[256,128]{1,0:T(8,128)(2,1)S(1)}, u32[]{:S(2)}, u32[]{:S(2)}) collective-permute-start(bf16[256,128]{1,0:T(8,128)(2,1)S(1)} %get-tuple-element.375), channel_id=1, source_target_pairs={{0,16},{16,32},{32,48},{48,64},{64,80},{80,96},{96,112},{112,128},... | collective-permute-start | bytes 196616 | tf_op jit(solution)/shard_map/while/body/eval_jaxpr/ppermute | solution.py:13
  104.2 8.9 %collective-permute-start = (bf16[256,128]{1,0:T(8,128)(2,1)S(1)}, bf16[256,128]{1,0:T(8,128)(2,1)S(1)}, u32[]{:S(2)}, u32[]{:S(2)}) collective-permute-start(bf16[256,128]{1,0:T(8,128)(2,1)S(1)} %get-tuple-element.374), channel_id=1, source_target_pairs={{0,16},{16,32},{32,48},{48,64},{64,80},{80,96},{96,112},{112,128},... | collective-permute-start | bytes 196616 | tf_op jit(solution)/shard_map/while/body/eval_jaxpr/ppermute | solution.py:13
  113.2 8.3 %collective-permute-start.1 = (bf16[256,128]{1,0:T(8,128)(2,1)S(1)}, bf16[256,128]{1,0:T(8,128)(2,1)S(1)}, u32[]{:S(2)}, u32[]{:S(2)}) collective-permute-start(bf16[256,128]{1,0:T(8,128)(2,1)S(1)} %get-tuple-element.375), channel_id=1, source_target_pairs={{0,16},{16,32},{32,48},{48,64},{64,80},{80,96},{96,112},{112,128},... | collective-permute-start | bytes 196616 | tf_op jit(solution)/shard_map/while/body/eval_jaxpr/ppermute | solution.py:13
  115.1 8.3 %collective-permute-start = (bf16[256,128]{1,0:T(8,128)(2,1)S(1)}, bf16[256,128]{1,0:T(8,128)(2,1)S(1)}, u32[]{:S(2)}, u32[]{:S(2)}) collective-permute-start(bf16[256,128]{1,0:T(8,128)(2,1)S(1)} %get-tuple-element.374), channel_id=1, source_target_pairs={{0,16},{16,32},{32,48},{48,64},{64,80},{80,96},{96,112},{112,128},... | collective-permute-start | bytes 196616 | tf_op jit(solution)/shard_map/while/body/eval_jaxpr/ppermute | solution.py:13
  123.4 8.9 %collective-permute-start.1 = (bf16[256,128]{1,0:T(8,128)(2,1)S(1)}, bf16[256,128]{1,0:T(8,128)(2,1)S(1)}, u32[]{:S(2)}, u32[]{:S(2)}) collective-permute-start(bf16[256,128]{1,0:T(8,128)(2,1)S(1)} %get-tuple-element.375), channel_id=1, source_target_pairs={{0,16},{16,32},{32,48},{48,64},{64,80},{80,96},{96,112},{112,128},... | collective-permute-start | bytes 196616 | tf_op jit(solution)/shard_map/while/body/eval_jaxpr/ppermute | solution.py:13
  125.4 8.3 %collective-permute-start = (bf16[256,128]{1,0:T(8,128)(2,1)S(1)}, bf16[256,128]{1,0:T(8,128)(2,1)S(1)}, u32[]{:S(2)}, u32[]{:S(2)}) collective-permute-start(bf16[256,128]{1,0:T(8,128)(2,1)S(1)} %get-tuple-element.374), channel_id=1, source_target_pairs={{0,16},{16,32},{32,48},{48,64},{64,80},{80,96},{96,112},{112,128},... | collective-permute-start | bytes 196616 | tf_op jit(solution)/shard_map/while/body/eval_jaxpr/ppermute | solution.py:13
  133.7 8.7 %collective-permute-start.1 = (bf16[256,128]{1,0:T(8,128)(2,1)S(1)}, bf16[256,128]{1,0:T(8,128)(2,1)S(1)}, u32[]{:S(2)}, u32[]{:S(2)}) collective-permute-start(bf16[256,128]{1,0:T(8,128)(2,1)S(1)} %get-tuple-element.375), channel_id=1, source_target_pairs={{0,16},{16,32},{32,48},{48,64},{64,80},{80,96},{96,112},{112,128},... | collective-permute-start | bytes 196616 | tf_op jit(solution)/shard_map/while/body/eval_jaxpr/ppermute | solution.py:13
  135.6 8.3 %collective-permute-start = (bf16[256,128]{1,0:T(8,128)(2,1)S(1)}, bf16[256,128]{1,0:T(8,128)(2,1)S(1)}, u32[]{:S(2)}, u32[]{:S(2)}) collective-permute-start(bf16[256,128]{1,0:T(8,128)(2,1)S(1)} %get-tuple-element.374), channel_id=1, source_target_pairs={{0,16},{16,32},{32,48},{48,64},{64,80},{80,96},{96,112},{112,128},... | collective-permute-start | bytes 196616 | tf_op jit(solution)/shard_map/while/body/eval_jaxpr/ppermute | solution.py:13
  143.9 8.3 %collective-permute-start.1 = (bf16[256,128]{1,0:T(8,128)(2,1)S(1)}, bf16[256,128]{1,0:T(8,128)(2,1)S(1)}, u32[]{:S(2)}, u32[]{:S(2)}) collective-permute-start(bf16[256,128]{1,0:T(8,128)(2,1)S(1)} %get-tuple-element.375), channel_id=1, source_target_pairs={{0,16},{16,32},{32,48},{48,64},{64,80},{80,96},{96,112},{112,128},... | collective-permute-start | bytes 196616 | tf_op jit(solution)/shard_map/while/body/eval_jaxpr/ppermute | solution.py:13
  145.9 8.3 %collective-permute-start = (bf16[256,128]{1,0:T(8,128)(2,1)S(1)}, bf16[256,128]{1,0:T(8,128)(2,1)S(1)}, u32[]{:S(2)}, u32[]{:S(2)}) collective-permute-start(bf16[256,128]{1,0:T(8,128)(2,1)S(1)} %get-tuple-element.374), channel_id=1, source_target_pairs={{0,16},{16,32},{32,48},{48,64},{64,80},{80,96},{96,112},{112,128},... | collective-permute-start | bytes 196616 | tf_op jit(solution)/shard_map/while/body/eval_jaxpr/ppermute | solution.py:13
  154.2 8.3 %collective-permute-start.1 = (bf16[256,128]{1,0:T(8,128)(2,1)S(1)}, bf16[256,128]{1,0:T(8,128)(2,1)S(1)}, u32[]{:S(2)}, u32[]{:S(2)}) collective-permute-start(bf16[256,128]{1,0:T(8,128)(2,1)S(1)} %get-tuple-element.375), channel_id=1, source_target_pairs={{0,16},{16,32},{32,48},{48,64},{64,80},{80,96},{96,112},{112,128},... | collective-permute-start | bytes 196616 | tf_op jit(solution)/shard_map/while/body/eval_jaxpr/ppermute | solution.py:13
  156.1 8.3 %collective-permute-start = (bf16[256,128]{1,0:T(8,128)(2,1)S(1)}, bf16[256,128]{1,0:T(8,128)(2,1)S(1)}, u32[]{:S(2)}, u32[]{:S(2)}) collective-permute-start(bf16[256,128]{1,0:T(8,128)(2,1)S(1)} %get-tuple-element.374), channel_id=1, source_target_pairs={{0,16},{16,32},{32,48},{48,64},{64,80},{80,96},{96,112},{112,128},... | collective-permute-start | bytes 196616 | tf_op jit(solution)/shard_map/while/body/eval_jaxpr/ppermute | solution.py:13
  164.4 8.3 %collective-permute-start.1 = (bf16[256,128]{1,0:T(8,128)(2,1)S(1)}, bf16[256,128]{1,0:T(8,128)(2,1)S(1)}, u32[]{:S(2)}, u32[]{:S(2)}) collective-permute-start(bf16[256,128]{1,0:T(8,128)(2,1)S(1)} %get-tuple-element.375), channel_id=1, source_target_pairs={{0,16},{16,32},{32,48},{48,64},{64,80},{80,96},{96,112},{112,128},... | collective-permute-start | bytes 196616 | tf_op jit(solution)/shard_map/while/body/eval_jaxpr/ppermute | solution.py:13
  166.4 8.3 %collective-permute-start = (bf16[256,128]{1,0:T(8,128)(2,1)S(1)}, bf16[256,128]{1,0:T(8,128)(2,1)S(1)}, u32[]{:S(2)}, u32[]{:S(2)}) collective-permute-start(bf16[256,128]{1,0:T(8,128)(2,1)S(1)} %get-tuple-element.374), channel_id=1, source_target_pairs={{0,16},{16,32},{32,48},{48,64},{64,80},{80,96},{96,112},{112,128},... | collective-permute-start | bytes 196616 | tf_op jit(solution)/shard_map/while/body/eval_jaxpr/ppermute | solution.py:13
  174.7 8.3 %collective-permute-start.1 = (bf16[256,128]{1,0:T(8,128)(2,1)S(1)}, bf16[256,128]{1,0:T(8,128)(2,1)S(1)}, u32[]{:S(2)}, u32[]{:S(2)}) collective-permute-start(bf16[256,128]{1,0:T(8,128)(2,1)S(1)} %get-tuple-element.375), channel_id=1, source_target_pairs={{0,16},{16,32},{32,48},{48,64},{64,80},{80,96},{96,112},{112,128},... | collective-permute-start | bytes 196616 | tf_op jit(solution)/shard_map/while/body/eval_jaxpr/ppermute | solution.py:13
  176.6 8.3 %collective-permute-start = (bf16[256,128]{1,0:T(8,128)(2,1)S(1)}, bf16[256,128]{1,0:T(8,128)(2,1)S(1)}, u32[]{:S(2)}, u32[]{:S(2)}) collective-permute-start(bf16[256,128]{1,0:T(8,128)(2,1)S(1)} %get-tuple-element.374), channel_id=1, source_target_pairs={{0,16},{16,32},{32,48},{48,64},{64,80},{80,96},{96,112},{112,128},... | collective-permute-start | bytes 196616 | tf_op jit(solution)/shard_map/while/body/eval_jaxpr/ppermute | solution.py:13
  212.2 90.8 %all-gather.3.cloned.1.call-start = ((), (), s32[]{:S(2)}) async-start(), calls=%async_computation.4 | async-start | bytes 2785280 | tf_op jit(solution)/shard_map/all_gather | solution.py:109
  232.9 142.4 %reduce-scatter.4.cloned.1.call-start = ((), (), s32[]{:S(2)}) async-start(), calls=%async_computation.6 | async-start | bytes 2785280
  377.0 20.0 %all-to-all-start.2 = ((bf16[128,32,20]{0,2,1:T(8,128)(2,1)}), bf16[128,32,20]{0,2,1:T(8,128)(2,1)S(1)}, u32[]{:S(2)}, u32[]{:S(2)}) async-start(bf16[128,32,20]{0,2,1:T(8,128)(2,1)} %all_to_all.30), calls=%async_computation.2 | async-start | bytes 393216 | tf_op jit(solution)/shard_map/all_to_all | solution.py:130
  412.9 6.8 %collective-permute-start.3 = (bf16[256,128]{1,0:T(8,128)(2,1)S(1)}, bf16[256,128]{1,0:T(8,128)(2,1)S(1)}, u32[]{:S(2)}, u32[]{:S(2)}) collective-permute-start(bf16[256,128]{1,0:T(8,128)(2,1)S(1)} %get-tuple-element.398), channel_id=1, source_target_pairs={{16,0},{32,16},{48,32},{64,48},{80,64},{96,80},{112,96},{128,112},... | collective-permute-start | bytes 196616 | tf_op jit(solution)/shard_map/while/body/eval_jaxpr/ppermute | solution.py:13
  422.3 7.7 %collective-permute-start.3 = (bf16[256,128]{1,0:T(8,128)(2,1)S(1)}, bf16[256,128]{1,0:T(8,128)(2,1)S(1)}, u32[]{:S(2)}, u32[]{:S(2)}) collective-permute-start(bf16[256,128]{1,0:T(8,128)(2,1)S(1)} %get-tuple-element.398), channel_id=1, source_target_pairs={{16,0},{32,16},{48,32},{64,48},{80,64},{96,80},{112,96},{128,112},... | collective-permute-start | bytes 196616 | tf_op jit(solution)/shard_map/while/body/eval_jaxpr/ppermute | solution.py:13
  428.0 6.2 %collective-permute-start.2 = (bf16[256,128]{1,0:T(8,128)(2,1)S(1)}, bf16[256,128]{1,0:T(8,128)(2,1)S(1)}, u32[]{:S(2)}, u32[]{:S(2)}) collective-permute-start(bf16[256,128]{1,0:T(8,128)(2,1)S(1)} %get-tuple-element.397), channel_id=1, source_target_pairs={{16,0},{32,16},{48,32},{64,48},{80,64},{96,80},{112,96},{128,112},... | collective-permute-start | bytes 196616 | tf_op jit(solution)/shard_map/while/body/eval_jaxpr/ppermute | solution.py:13
  434.2 6.2 %collective-permute-start.3 = (bf16[256,128]{1,0:T(8,128)(2,1)S(1)}, bf16[256,128]{1,0:T(8,128)(2,1)S(1)}, u32[]{:S(2)}, u32[]{:S(2)}) collective-permute-start(bf16[256,128]{1,0:T(8,128)(2,1)S(1)} %get-tuple-element.398), channel_id=1, source_target_pairs={{16,0},{32,16},{48,32},{64,48},{80,64},{96,80},{112,96},{128,112},... | collective-permute-start | bytes 196616 | tf_op jit(solution)/shard_map/while/body/eval_jaxpr/ppermute | solution.py:13
  444.6 6.6 %collective-permute-start.3 = (bf16[256,128]{1,0:T(8,128)(2,1)S(1)}, bf16[256,128]{1,0:T(8,128)(2,1)S(1)}, u32[]{:S(2)}, u32[]{:S(2)}) collective-permute-start(bf16[256,128]{1,0:T(8,128)(2,1)S(1)} %get-tuple-element.398), channel_id=1, source_target_pairs={{16,0},{32,16},{48,32},{64,48},{80,64},{96,80},{112,96},{128,112},... | collective-permute-start | bytes 196616 | tf_op jit(solution)/shard_map/while/body/eval_jaxpr/ppermute | solution.py:13
  448.6 6.6 %collective-permute-start.2 = (bf16[256,128]{1,0:T(8,128)(2,1)S(1)}, bf16[256,128]{1,0:T(8,128)(2,1)S(1)}, u32[]{:S(2)}, u32[]{:S(2)}) collective-permute-start(bf16[256,128]{1,0:T(8,128)(2,1)S(1)} %get-tuple-element.397), channel_id=1, source_target_pairs={{16,0},{32,16},{48,32},{64,48},{80,64},{96,80},{112,96},{128,112},... | collective-permute-start | bytes 196616 | tf_op jit(solution)/shard_map/while/body/eval_jaxpr/ppermute | solution.py:13
  465.7 6.4 %collective-permute-start.3 = (bf16[256,128]{1,0:T(8,128)(2,1)S(1)}, bf16[256,128]{1,0:T(8,128)(2,1)S(1)}, u32[]{:S(2)}, u32[]{:S(2)}) collective-permute-start(bf16[256,128]{1,0:T(8,128)(2,1)S(1)} %get-tuple-element.398), channel_id=1, source_target_pairs={{16,0},{32,16},{48,32},{64,48},{80,64},{96,80},{112,96},{128,112},... | collective-permute-start | bytes 196616 | tf_op jit(solution)/shard_map/while/body/eval_jaxpr/ppermute | solution.py:13
  475.9 6.2 %collective-permute-start.3 = (bf16[256,128]{1,0:T(8,128)(2,1)S(1)}, bf16[256,128]{1,0:T(8,128)(2,1)S(1)}, u32[]{:S(2)}, u32[]{:S(2)}) collective-permute-start(bf16[256,128]{1,0:T(8,128)(2,1)S(1)} %get-tuple-element.398), channel_id=1, source_target_pairs={{16,0},{32,16},{48,32},{64,48},{80,64},{96,80},{112,96},{128,112},... | collective-permute-start | bytes 196616 | tf_op jit(solution)/shard_map/while/body/eval_jaxpr/ppermute | solution.py:13
  496.4 6.8 %collective-permute-start.3 = (bf16[256,128]{1,0:T(8,128)(2,1)S(1)}, bf16[256,128]{1,0:T(8,128)(2,1)S(1)}, u32[]{:S(2)}, u32[]{:S(2)}) collective-permute-start(bf16[256,128]{1,0:T(8,128)(2,1)S(1)} %get-tuple-element.398), channel_id=1, source_target_pairs={{16,0},{32,16},{48,32},{64,48},{80,64},{96,80},{112,96},{128,112},... | collective-permute-start | bytes 196616 | tf_op jit(solution)/shard_map/while/body/eval_jaxpr/ppermute | solution.py:13
  510.7 6.6 %collective-permute-start.2 = (bf16[256,128]{1,0:T(8,128)(2,1)S(1)}, bf16[256,128]{1,0:T(8,128)(2,1)S(1)}, u32[]{:S(2)}, u32[]{:S(2)}) collective-permute-start(bf16[256,128]{1,0:T(8,128)(2,1)S(1)} %get-tuple-element.397), channel_id=1, source_target_pairs={{16,0},{32,16},{48,32},{64,48},{80,64},{96,80},{112,96},{128,112},... | collective-permute-start | bytes 196616 | tf_op jit(solution)/shard_map/while/body/eval_jaxpr/ppermute | solution.py:13
  537.3 7.0 %collective-permute-start.3 = (bf16[256,128]{1,0:T(8,128)(2,1)S(1)}, bf16[256,128]{1,0:T(8,128)(2,1)S(1)}, u32[]{:S(2)}, u32[]{:S(2)}) collective-permute-start(bf16[256,128]{1,0:T(8,128)(2,1)S(1)} %get-tuple-element.398), channel_id=1, source_target_pairs={{16,0},{32,16},{48,32},{64,48},{80,64},{96,80},{112,96},{128,112},... | collective-permute-start | bytes 196616 | tf_op jit(solution)/shard_map/while/body/eval_jaxpr/ppermute | solution.py:13
  541.9 6.7 %collective-permute-start.2 = (bf16[256,128]{1,0:T(8,128)(2,1)S(1)}, bf16[256,128]{1,0:T(8,128)(2,1)S(1)}, u32[]{:S(2)}, u32[]{:S(2)}) collective-permute-start(bf16[256,128]{1,0:T(8,128)(2,1)S(1)} %get-tuple-element.397), channel_id=1, source_target_pairs={{16,0},{32,16},{48,32},{64,48},{80,64},{96,80},{112,96},{128,112},... | collective-permute-start | bytes 196616 | tf_op jit(solution)/shard_map/while/body/eval_jaxpr/ppermute | solution.py:13
  (30 other events, 405.7 us)
Sparse Core Ops, SparseCore 0:
  212.3 43.3 all-gather.4
  258.4 44.5 all-gather.2
  313.7 61.4 reduce-scatter.3
where the time goes:
time: 590 us; the launch traced here: 587 us
  waiting for transfers between devices  277 us (47%)
  starting transfers between devices  183 us (31%)
  matrix products  35.4 us (6%)
  blocking collectives  31.8 us (5%)
  local copies, waits for them, and re-layouts  21.9 us (4%)
  other arithmetic  21.3 us (4%)
  between operations  14.7 us (2%)
    ppermute x64, starting transfers between devices, shifted(): return lax.ppermute(block, axis, route)  173 us
    ppermute x64, waiting for transfers between devices, shifted(): return lax.ppermute(block, axis, route)  147 us
    unnamed x4, waiting for transfers between devices  57.7 us
    all_gather x1, waiting for transfers between devices, per_device(): full_grads = lax.all_gather(recv_grads, 'exp', axis=1, tiled=True)  43.8 us
    all_gather x1, waiting for transfers between devices, per_device(): full_tokens = lax.all_gather(recv_tokens, 'exp', axis=1, tiled=True)  22.8 us
    all_to_all x1, blocking collectives, per_device(): lax.all_to_all(send_grads, 'seq', split_axis=0, concat_axis=0, tiled=True)  15.9 us
    all_to_all x1, blocking collectives, per_device(): lax.all_to_all(send_tokens, 'seq', split_axis=0, concat_axis=0, tiled=True)  15.8 us
    add x16, other arithmetic, relay_grads(): value_acc + lax.dynamic_index_in_dim(value_parts, index, 0, keepdims=False)  14.7 us
  transfers between devices with their start and end apart: 68, of which 64 were waited for; matrix products, arithmetic and copies ran while one was open for 5% of the time, Pallas kernels for 0%

commit v1 on v0

--- a/solution.py
+++ b/solution.py
@@ -106,7 +106,21 @@
     weight_out = expert_out[0]
     full_tokens = lax.all_gather(recv_tokens, "exp", axis=1, tiled=True)
     pre_act = jnp.dot(full_tokens, weight_in, preferred_element_type=jnp.float32)
-    full_grads = lax.all_gather(recv_grads, "exp", axis=1, tiled=True)
+    ways, here, hop = (lax.axis_size("exp"), lax.axis_index("exp"), recv_grads.shape[1])
+    shape = [n * ways if d == 1 else n for d, n in enumerate(recv_grads.shape)]
+    full = lax.dynamic_update_slice_in_dim(
+        jnp.zeros(shape, recv_grads.dtype), recv_grads, here * hop, axis=1
+    )
+    going_up = going_down = recv_grads
+    for far in range(1, ways // 2 + 1):
+        going_up = lax.ppermute(going_up, "exp", [(d, (d + 1) % ways) for d in range(ways)])
+        full = lax.dynamic_update_slice_in_dim(full, going_up, (here - far) % ways * hop, axis=1)
+        if 2 * far < ways:
+            going_down = lax.ppermute(going_down, "exp", [(d, (d - 1) % ways) for d in range(ways)])
+            full = lax.dynamic_update_slice_in_dim(
+                full, going_down, (here + far) % ways * hop, axis=1
+            )
+    full_grads = full
     logistic = jax.nn.sigmoid(pre_act)
     hidden = (pre_act * logistic).astype(jnp.bfloat16)
     through_out = lax.dot_general(

time: 590 us -> 577 us (0.978)
  waiting for transfers between devices: 277 us -> 241 us
  starting transfers between devices: 183 us -> 204 us
  local copies, waits for them, and re-layouts: 21.9 us -> 30.4 us
    all_gather x1 -> x0, waiting for transfers between devices: 43.8 us -> none  [per_device(): full_grads = lax.all_gather(recv_grads, 'exp', axis=1, tiled=True)]
    all_gather x1, waiting for transfers between devices: 22.8 us -> 0.01 us  [per_device(): full_tokens = lax.all_gather(recv_tokens, 'exp', axis=1, tiled=True)]
    ppermute x0 -> x15, starting transfers between devices: none -> 21.5 us  [the longest x7 21.5 us: per_device(): lax.ppermute(going_down, 'exp', [(d, (d - 1) % ways) for d in range(ways)])]
    ppermute x0 -> x15, waiting for transfers between devices: none -> 17 us  [the longest x8 16.4 us: per_device(): lax.ppermute(going_up, 'exp', [(d, (d + 1) % ways) for d in range(ways)])]
    ppermute x64, waiting for transfers between devices: 147 us -> 161 us  [shifted(): return lax.ppermute(block, axis, route)]
    dynamic_update_slice x0 -> x16, local copies, waits for them, and re-layouts: none -> 11.2 us  [the longest x8 5.65 us: per_device(): lax.dynamic_update_slice_in_dim(full, going_up, (here - far) % ways * hop...]
    unnamed x4 -> x3, waiting for transfers between devices: 57.7 us -> 57 us
  transfers between devices with their start and end apart: 68 -> 82, of which waited for: 64 -> 73; matrix products, arithmetic and copies ran while one was open for 5% -> 4% of each run, Pallas kernels for 0% -> 0%
where the time goes in v1:
time: 577 us; the launch traced here: 575 us
  waiting for transfers between devices  241 us (42%)
  starting transfers between devices  204 us (35%)
  matrix products  32.7 us (6%)
  local copies, waits for them, and re-layouts  30.4 us (5%)
  blocking collectives  30.3 us (5%)
  other arithmetic  19.6 us (3%)
  between operations  15.1 us (3%)
    ppermute x64, starting transfers between devices, shifted(): return lax.ppermute(block, axis, route)  172 us
    ppermute x64, waiting for transfers between devices, shifted(): return lax.ppermute(block, axis, route)  161 us
    unnamed x3, waiting for transfers between devices  57 us
    ppermute x7, starting transfers between devices, per_device(): lax.ppermute(going_down, 'exp', [(d, (d - 1) % ways) for d in range(ways)])  21.5 us
    ppermute x8, waiting for transfers between devices, per_device(): lax.ppermute(going_up, 'exp', [(d, (d + 1) % ways) for d in range(ways)])  16.4 us
    all_to_all x1, blocking collectives, per_device(): lax.all_to_all(send_tokens, 'seq', split_axis=0, concat_axis=0, tiled=True)  15.9 us
    add x16, other arithmetic, relay_grads(): value_acc + lax.dynamic_index_in_dim(value_parts, index, 0, keepdims=False)  14.7 us
    all_to_all x1, blocking collectives, per_device(): lax.all_to_all(send_grads, 'seq', split_axis=0, concat_axis=0, tiled=True)  14.4 us
  transfers between devices with their start and end apart: 82, of which 73 were waited for; matrix products, arithmetic and copies ran while one was open for 4% of the time, Pallas kernels for 0%

profile of v1, /device:TPU:2, one launch (start us, length us, event | category | flops | bytes accessed | tf_op | source)
XLA Modules:
  0.0 574.7 jit_solution(11461478918284558488)
XLA Ops:
  14.8 170.1 %while.36 = (s32[]{:T(128)}, bf16[17,256,128]{2,1,0:T(8,128)(2,1)S(1)}, bf16[17,256,128]{2,1,0:T(8,128)(2,1)S(1)}, bf16[256,128]{1,0:T(8,128)(2,1)S(1)}, bf16[25...) while((s32[]{:T(128)}, bf16[17,256,128]{2,1,0:T(8,128)(2,1)S(1)}, ...), condition=%wide.region_1.2_spmd, body=%wide.region_0.1_spmd.sunk | while | flops 5 | bytes 1048791 | solution.py:74
  14.8 4.3 collective-permute-start
  19.1 4.3 collective-permute-start.1
  23.4 4.6 collective-permute-done
  52.4 4.0 collective-permute-start.1
  85.1 4.4 collective-permute-done
  95.4 4.4 collective-permute-done
  106.2 5.0 collective-permute-done
  117.1 4.4 collective-permute-done
  127.3 5.0 collective-permute-done
  137.6 4.8 collective-permute-done
  147.8 4.4 collective-permute-done
  158.1 4.4 collective-permute-done
  168.3 4.4 collective-permute-done
  178.6 4.4 collective-permute-done
  185.0 6.0 %fusion.71 = (f32[256]{0:T(256)S(1)}, f32[256,4352]{0,1:T(8,128)S(1)}) fusion(f32[]{:T(128)} %bitcast.116, bf16[4352,128]{1,0:T(8,128)(2,1)S(1)} %bitcast.121, bf16[256,128]{1,0:T(8,128)(2,1)} %param.13, s32[]{:T(128)S(6)} %axis_index.23, s32[4352]{0:T(1024)} %get-tuple-element.295, s32[4352]{0:T(1024)} %get-tuple-element.298, ...), kind=kOutput, calls=%fused_computation.120 | convolution fusion | flops 304152320 | bytes 5715464 | tf_op jit(solution)/shard_map/ihd,jhd->hij/dot_general | solution.py:20
  193.5 15.9 %all_to_all.36 = bf16[32,20,128]{2,1,0:T(8,128)(2,1)S(1)} all-to-all(bf16[32,20,128]{2,1,0:T(8,128)(2,1)S(1)} %all_to_all.27), channel_id=1, replica_groups=mesh['seq'=32,'exp'=16] {'seq'}, dimensions={0} | all-to-all | bytes 327680 | tf_op jit(solution)/shard_map/all_to_all | solution.py:102
  210.8 14.4 %all_to_all.37 = bf16[32,20,128]{2,1,0:T(8,128)(2,1)S(1)} all-to-all(bf16[32,20,128]{2,1,0:T(8,128)(2,1)S(1)} %all_to_all.24), channel_id=1, replica_groups=mesh['seq'=32,'exp'=16] {'seq'}, dimensions={0} | all-to-all | bytes 327680 | tf_op jit(solution)/shard_map/all_to_all | solution.py:103
  271.5 4.5 collective-permute-done.18
  284.5 4.4 copy.33
  292.7 56.9 %reduce-scatter.4.cloned.1.call-done = bf16[128,640]{1,0:T(8,128)(2,1)} async-done(((bf16[2048,640]{1,0:T(8,128)(2,1)}), bf16[128,640]{1,0:T(8,128)(2,1)}) %reduce-scatter.4.cloned.1.call-update) | async-done | bytes 163856
  351.5 10.5 %all-to-all-start.2 = ((bf16[128,32,20]{0,2,1:T(8,128)(2,1)}), bf16[128,32,20]{0,2,1:T(8,128)(2,1)S(1)}, u32[]{:S(2)}, u32[]{:S(2)}) async-start(bf16[128,32,20]{0,2,1:T(8,128)(2,1)} %all_to_all.30), calls=%async_computation.2 | async-start | bytes 393216 | tf_op jit(solution)/shard_map/all_to_all | solution.py:144
  365.7 5.7 all-to-all-done.2
  372.1 4.6 convolution_bitcast_fusion
  386.8 180.4 %while.37 = (s32[]{:T(128)}, bf16[256,128]{1,0:T(8,128)(2,1)S(1)}, bf16[256,128]{1,0:T(8,128)(2,1)S(1)}, f32[17,256,128]{2,1,0:T(8,128)S(1)}, f32[17,256,128]{2,...) while((s32[]{:T(128)}, bf16[256,128]{1,0:T(8,128)(2,1)S(1)}, ...), condition=%wide.region_9.10_spmd, body=%wide.region_8.9_spmd.sunk | while | flops 196614 | bytes 1048803 | solution.py:180
  397.5 5.2 collective-permute-start.2
  404.7 4.2 collective-permute-done.3
  409.8 4.0 collective-permute-start.2
  416.0 4.0 collective-permute-done.3
  421.0 4.4 collective-permute-start.2
  427.3 4.5 collective-permute-done.3
  443.6 4.3 collective-permute-start.2
  449.9 4.2 collective-permute-done.3
  455.0 4.0 collective-permute-start.2
  461.2 4.0 collective-permute-done.3
  466.2 4.0 collective-permute-start.2
  472.3 4.0 collective-permute-done.3
  477.3 4.0 collective-permute-start.2
  488.4 4.0 collective-permute-start.2
  494.6 4.2 collective-permute-done.3
  521.8 4.1 collective-permute-start.2
  528.0 4.1 collective-permute-done.3
  533.0 4.2 collective-permute-start.2
  539.9 4.0 collective-permute-done.3
  544.8 4.2 collective-permute-start.2
  551.0 4.1 collective-permute-done.3
  556.1 4.0 collective-permute-start.2
  562.3 4.0 collective-permute-done.3
  (312 shorter events, 276.5 us)
Async XLA Ops:
  7.2 269.5 %all-gather.2.cloned.1.call-start = ((), (), s32[]{:S(2)}) async-start(), calls=%async_computation.4 | async-start | bytes 2785280 | tf_op jit(solution)/shard_map/all_gather | solution.py:107
  14.8 13.2 %collective-permute-start = (bf16[256,128]{1,0:T(8,128)(2,1)S(1)}, bf16[256,128]{1,0:T(8,128)(2,1)S(1)}, u32[]{:S(2)}, u32[]{:S(2)}) collective-permute-start(bf16[256,128]{1,0:T(8,128)(2,1)S(1)} %get-tuple-element.374), channel_id=1, source_target_pairs={{0,16},{16,32},{32,48},{48,64},{64,80},{80,96},{96,112},{112,128},... | collective-permute-start | bytes 196616 | tf_op jit(solution)/shard_map/while/body/eval_jaxpr/ppermute | solution.py:13
  19.1 10.8 %collective-permute-start.1 = (bf16[256,128]{1,0:T(8,128)(2,1)S(1)}, bf16[256,128]{1,0:T(8,128)(2,1)S(1)}, u32[]{:S(2)}, u32[]{:S(2)}) collective-permute-start(bf16[256,128]{1,0:T(8,128)(2,1)S(1)} %get-tuple-element.375), channel_id=1, source_target_pairs={{0,16},{16,32},{32,48},{48,64},{64,80},{80,96},{96,112},{112,128},... | collective-permute-start | bytes 196616 | tf_op jit(solution)/shard_map/while/body/eval_jaxpr/ppermute | solution.py:13
  30.0 8.9 %collective-permute-start = (bf16[256,128]{1,0:T(8,128)(2,1)S(1)}, bf16[256,128]{1,0:T(8,128)(2,1)S(1)}, u32[]{:S(2)}, u32[]{:S(2)}) collective-permute-start(bf16[256,128]{1,0:T(8,128)(2,1)S(1)} %get-tuple-element.374), channel_id=1, source_target_pairs={{0,16},{16,32},{32,48},{48,64},{64,80},{80,96},{96,112},{112,128},... | collective-permute-start | bytes 196616 | tf_op jit(solution)/shard_map/while/body/eval_jaxpr/ppermute | solution.py:13
  31.9 8.3 %collective-permute-start.1 = (bf16[256,128]{1,0:T(8,128)(2,1)S(1)}, bf16[256,128]{1,0:T(8,128)(2,1)S(1)}, u32[]{:S(2)}, u32[]{:S(2)}) collective-permute-start(bf16[256,128]{1,0:T(8,128)(2,1)S(1)} %get-tuple-element.375), channel_id=1, source_target_pairs={{0,16},{16,32},{32,48},{48,64},{64,80},{80,96},{96,112},{112,128},... | collective-permute-start | bytes 196616 | tf_op jit(solution)/shard_map/while/body/eval_jaxpr/ppermute | solution.py:13
  40.2 8.7 %collective-permute-start = (bf16[256,128]{1,0:T(8,128)(2,1)S(1)}, bf16[256,128]{1,0:T(8,128)(2,1)S(1)}, u32[]{:S(2)}, u32[]{:S(2)}) collective-permute-start(bf16[256,128]{1,0:T(8,128)(2,1)S(1)} %get-tuple-element.374), channel_id=1, source_target_pairs={{0,16},{16,32},{32,48},{48,64},{64,80},{80,96},{96,112},{112,128},... | collective-permute-start | bytes 196616 | tf_op jit(solution)/shard_map/while/body/eval_jaxpr/ppermute | solution.py:13
  42.2 8.3 %collective-permute-start.1 = (bf16[256,128]{1,0:T(8,128)(2,1)S(1)}, bf16[256,128]{1,0:T(8,128)(2,1)S(1)}, u32[]{:S(2)}, u32[]{:S(2)}) collective-permute-start(bf16[256,128]{1,0:T(8,128)(2,1)S(1)} %get-tuple-element.375), channel_id=1, source_target_pairs={{0,16},{16,32},{32,48},{48,64},{64,80},{80,96},{96,112},{112,128},... | collective-permute-start | bytes 196616 | tf_op jit(solution)/shard_map/while/body/eval_jaxpr/ppermute | solution.py:13
  50.5 8.3 %collective-permute-start = (bf16[256,128]{1,0:T(8,128)(2,1)S(1)}, bf16[256,128]{1,0:T(8,128)(2,1)S(1)}, u32[]{:S(2)}, u32[]{:S(2)}) collective-permute-start(bf16[256,128]{1,0:T(8,128)(2,1)S(1)} %get-tuple-element.374), channel_id=1, source_target_pairs={{0,16},{16,32},{32,48},{48,64},{64,80},{80,96},{96,112},{112,128},... | collective-permute-start | bytes 196616 | tf_op jit(solution)/shard_map/while/body/eval_jaxpr/ppermute | solution.py:13
  52.4 8.3 %collective-permute-start.1 = (bf16[256,128]{1,0:T(8,128)(2,1)S(1)}, bf16[256,128]{1,0:T(8,128)(2,1)S(1)}, u32[]{:S(2)}, u32[]{:S(2)}) collective-permute-start(bf16[256,128]{1,0:T(8,128)(2,1)S(1)} %get-tuple-element.375), channel_id=1, source_target_pairs={{0,16},{16,32},{32,48},{48,64},{64,80},{80,96},{96,112},{112,128},... | collective-permute-start | bytes 196616 | tf_op jit(solution)/shard_map/while/body/eval_jaxpr/ppermute | solution.py:13
  60.7 8.3 %collective-permute-start = (bf16[256,128]{1,0:T(8,128)(2,1)S(1)}, bf16[256,128]{1,0:T(8,128)(2,1)S(1)}, u32[]{:S(2)}, u32[]{:S(2)}) collective-permute-start(bf16[256,128]{1,0:T(8,128)(2,1)S(1)} %get-tuple-element.374), channel_id=1, source_target_pairs={{0,16},{16,32},{32,48},{48,64},{64,80},{80,96},{96,112},{112,128},... | collective-permute-start | bytes 196616 | tf_op jit(solution)/shard_map/while/body/eval_jaxpr/ppermute | solution.py:13
  62.7 8.3 %collective-permute-start.1 = (bf16[256,128]{1,0:T(8,128)(2,1)S(1)}, bf16[256,128]{1,0:T(8,128)(2,1)S(1)}, u32[]{:S(2)}, u32[]{:S(2)}) collective-permute-start(bf16[256,128]{1,0:T(8,128)(2,1)S(1)} %get-tuple-element.375), channel_id=1, source_target_pairs={{0,16},{16,32},{32,48},{48,64},{64,80},{80,96},{96,112},{112,128},... | collective-permute-start | bytes 196616 | tf_op jit(solution)/shard_map/while/body/eval_jaxpr/ppermute | solution.py:13
  71.0 8.3 %collective-permute-start = (bf16[256,128]{1,0:T(8,128)(2,1)S(1)}, bf16[256,128]{1,0:T(8,128)(2,1)S(1)}, u32[]{:S(2)}, u32[]{:S(2)}) collective-permute-start(bf16[256,128]{1,0:T(8,128)(2,1)S(1)} %get-tuple-element.374), channel_id=1, source_target_pairs={{0,16},{16,32},{32,48},{48,64},{64,80},{80,96},{96,112},{112,128},... | collective-permute-start | bytes 196616 | tf_op jit(solution)/shard_map/while/body/eval_jaxpr/ppermute | solution.py:13
  72.9 8.3 %collective-permute-start.1 = (bf16[256,128]{1,0:T(8,128)(2,1)S(1)}, bf16[256,128]{1,0:T(8,128)(2,1)S(1)}, u32[]{:S(2)}, u32[]{:S(2)}) collective-permute-start(bf16[256,128]{1,0:T(8,128)(2,1)S(1)} %get-tuple-element.375), channel_id=1, source_target_pairs={{0,16},{16,32},{32,48},{48,64},{64,80},{80,96},{96,112},{112,128},... | collective-permute-start | bytes 196616 | tf_op jit(solution)/shard_map/while/body/eval_jaxpr/ppermute | solution.py:13
  81.2 8.3 %collective-permute-start = (bf16[256,128]{1,0:T(8,128)(2,1)S(1)}, bf16[256,128]{1,0:T(8,128)(2,1)S(1)}, u32[]{:S(2)}, u32[]{:S(2)}) collective-permute-start(bf16[256,128]{1,0:T(8,128)(2,1)S(1)} %get-tuple-element.374), channel_id=1, source_target_pairs={{0,16},{16,32},{32,48},{48,64},{64,80},{80,96},{96,112},{112,128},... | collective-permute-start | bytes 196616 | tf_op jit(solution)/shard_map/while/body/eval_jaxpr/ppermute | solution.py:13
  83.2 8.3 %collective-permute-start.1 = (bf16[256,128]{1,0:T(8,128)(2,1)S(1)}, bf16[256,128]{1,0:T(8,128)(2,1)S(1)}, u32[]{:S(2)}, u32[]{:S(2)}) collective-permute-start(bf16[256,128]{1,0:T(8,128)(2,1)S(1)} %get-tuple-element.375), channel_id=1, source_target_pairs={{0,16},{16,32},{32,48},{48,64},{64,80},{80,96},{96,112},{112,128},... | collective-permute-start | bytes 196616 | tf_op jit(solution)/shard_map/while/body/eval_jaxpr/ppermute | solution.py:13
  91.5 8.3 %collective-permute-start = (bf16[256,128]{1,0:T(8,128)(2,1)S(1)}, bf16[256,128]{1,0:T(8,128)(2,1)S(1)}, u32[]{:S(2)}, u32[]{:S(2)}) collective-permute-start(bf16[256,128]{1,0:T(8,128)(2,1)S(1)} %get-tuple-element.374), channel_id=1, source_target_pairs={{0,16},{16,32},{32,48},{48,64},{64,80},{80,96},{96,112},{112,128},... | collective-permute-start | bytes 196616 | tf_op jit(solution)/shard_map/while/body/eval_jaxpr/ppermute | solution.py:13
  93.4 8.9 %collective-permute-start.1 = (bf16[256,128]{1,0:T(8,128)(2,1)S(1)}, bf16[256,128]{1,0:T(8,128)(2,1)S(1)}, u32[]{:S(2)}, u32[]{:S(2)}) collective-permute-start(bf16[256,128]{1,0:T(8,128)(2,1)S(1)} %get-tuple-element.375), channel_id=1, source_target_pairs={{0,16},{16,32},{32,48},{48,64},{64,80},{80,96},{96,112},{112,128},... | collective-permute-start | bytes 196616 | tf_op jit(solution)/shard_map/while/body/eval_jaxpr/ppermute | solution.py:13
  102.3 8.9 %collective-permute-start = (bf16[256,128]{1,0:T(8,128)(2,1)S(1)}, bf16[256,128]{1,0:T(8,128)(2,1)S(1)}, u32[]{:S(2)}, u32[]{:S(2)}) collective-permute-start(bf16[256,128]{1,0:T(8,128)(2,1)S(1)} %get-tuple-element.374), channel_id=1, source_target_pairs={{0,16},{16,32},{32,48},{48,64},{64,80},{80,96},{96,112},{112,128},... | collective-permute-start | bytes 196616 | tf_op jit(solution)/shard_map/while/body/eval_jaxpr/ppermute | solution.py:13
  104.3 8.9 %collective-permute-start.1 = (bf16[256,128]{1,0:T(8,128)(2,1)S(1)}, bf16[256,128]{1,0:T(8,128)(2,1)S(1)}, u32[]{:S(2)}, u32[]{:S(2)}) collective-permute-start(bf16[256,128]{1,0:T(8,128)(2,1)S(1)} %get-tuple-element.375), channel_id=1, source_target_pairs={{0,16},{16,32},{32,48},{48,64},{64,80},{80,96},{96,112},{112,128},... | collective-permute-start | bytes 196616 | tf_op jit(solution)/shard_map/while/body/eval_jaxpr/ppermute | solution.py:13
  113.2 8.3 %collective-permute-start = (bf16[256,128]{1,0:T(8,128)(2,1)S(1)}, bf16[256,128]{1,0:T(8,128)(2,1)S(1)}, u32[]{:S(2)}, u32[]{:S(2)}) collective-permute-start(bf16[256,128]{1,0:T(8,128)(2,1)S(1)} %get-tuple-element.374), channel_id=1, source_target_pairs={{0,16},{16,32},{32,48},{48,64},{64,80},{80,96},{96,112},{112,128},... | collective-permute-start | bytes 196616 | tf_op jit(solution)/shard_map/while/body/eval_jaxpr/ppermute | solution.py:13
  115.1 8.3 %collective-permute-start.1 = (bf16[256,128]{1,0:T(8,128)(2,1)S(1)}, bf16[256,128]{1,0:T(8,128)(2,1)S(1)}, u32[]{:S(2)}, u32[]{:S(2)}) collective-permute-start(bf16[256,128]{1,0:T(8,128)(2,1)S(1)} %get-tuple-element.375), channel_id=1, source_target_pairs={{0,16},{16,32},{32,48},{48,64},{64,80},{80,96},{96,112},{112,128},... | collective-permute-start | bytes 196616 | tf_op jit(solution)/shard_map/while/body/eval_jaxpr/ppermute | solution.py:13
  123.5 8.9 %collective-permute-start = (bf16[256,128]{1,0:T(8,128)(2,1)S(1)}, bf16[256,128]{1,0:T(8,128)(2,1)S(1)}, u32[]{:S(2)}, u32[]{:S(2)}) collective-permute-start(bf16[256,128]{1,0:T(8,128)(2,1)S(1)} %get-tuple-element.374), channel_id=1, source_target_pairs={{0,16},{16,32},{32,48},{48,64},{64,80},{80,96},{96,112},{112,128},... | collective-permute-start | bytes 196616 | tf_op jit(solution)/shard_map/while/body/eval_jaxpr/ppermute | solution.py:13
  125.4 8.3 %collective-permute-start.1 = (bf16[256,128]{1,0:T(8,128)(2,1)S(1)}, bf16[256,128]{1,0:T(8,128)(2,1)S(1)}, u32[]{:S(2)}, u32[]{:S(2)}) collective-permute-start(bf16[256,128]{1,0:T(8,128)(2,1)S(1)} %get-tuple-element.375), channel_id=1, source_target_pairs={{0,16},{16,32},{32,48},{48,64},{64,80},{80,96},{96,112},{112,128},... | collective-permute-start | bytes 196616 | tf_op jit(solution)/shard_map/while/body/eval_jaxpr/ppermute | solution.py:13
  133.7 8.7 %collective-permute-start = (bf16[256,128]{1,0:T(8,128)(2,1)S(1)}, bf16[256,128]{1,0:T(8,128)(2,1)S(1)}, u32[]{:S(2)}, u32[]{:S(2)}) collective-permute-start(bf16[256,128]{1,0:T(8,128)(2,1)S(1)} %get-tuple-element.374), channel_id=1, source_target_pairs={{0,16},{16,32},{32,48},{48,64},{64,80},{80,96},{96,112},{112,128},... | collective-permute-start | bytes 196616 | tf_op jit(solution)/shard_map/while/body/eval_jaxpr/ppermute | solution.py:13
  135.6 8.3 %collective-permute-start.1 = (bf16[256,128]{1,0:T(8,128)(2,1)S(1)}, bf16[256,128]{1,0:T(8,128)(2,1)S(1)}, u32[]{:S(2)}, u32[]{:S(2)}) collective-permute-start(bf16[256,128]{1,0:T(8,128)(2,1)S(1)} %get-tuple-element.375), channel_id=1, source_target_pairs={{0,16},{16,32},{32,48},{48,64},{64,80},{80,96},{96,112},{112,128},... | collective-permute-start | bytes 196616 | tf_op jit(solution)/shard_map/while/body/eval_jaxpr/ppermute | solution.py:13
  144.0 8.3 %collective-permute-start = (bf16[256,128]{1,0:T(8,128)(2,1)S(1)}, bf16[256,128]{1,0:T(8,128)(2,1)S(1)}, u32[]{:S(2)}, u32[]{:S(2)}) collective-permute-start(bf16[256,128]{1,0:T(8,128)(2,1)S(1)} %get-tuple-element.374), channel_id=1, source_target_pairs={{0,16},{16,32},{32,48},{48,64},{64,80},{80,96},{96,112},{112,128},... | collective-permute-start | bytes 196616 | tf_op jit(solution)/shard_map/while/body/eval_jaxpr/ppermute | solution.py:13
  145.9 8.3 %collective-permute-start.1 = (bf16[256,128]{1,0:T(8,128)(2,1)S(1)}, bf16[256,128]{1,0:T(8,128)(2,1)S(1)}, u32[]{:S(2)}, u32[]{:S(2)}) collective-permute-start(bf16[256,128]{1,0:T(8,128)(2,1)S(1)} %get-tuple-element.375), channel_id=1, source_target_pairs={{0,16},{16,32},{32,48},{48,64},{64,80},{80,96},{96,112},{112,128},... | collective-permute-start | bytes 196616 | tf_op jit(solution)/shard_map/while/body/eval_jaxpr/ppermute | solution.py:13
  154.2 8.3 %collective-permute-start = (bf16[256,128]{1,0:T(8,128)(2,1)S(1)}, bf16[256,128]{1,0:T(8,128)(2,1)S(1)}, u32[]{:S(2)}, u32[]{:S(2)}) collective-permute-start(bf16[256,128]{1,0:T(8,128)(2,1)S(1)} %get-tuple-element.374), channel_id=1, source_target_pairs={{0,16},{16,32},{32,48},{48,64},{64,80},{80,96},{96,112},{112,128},... | collective-permute-start | bytes 196616 | tf_op jit(solution)/shard_map/while/body/eval_jaxpr/ppermute | solution.py:13
  156.1 8.3 %collective-permute-start.1 = (bf16[256,128]{1,0:T(8,128)(2,1)S(1)}, bf16[256,128]{1,0:T(8,128)(2,1)S(1)}, u32[]{:S(2)}, u32[]{:S(2)}) collective-permute-start(bf16[256,128]{1,0:T(8,128)(2,1)S(1)} %get-tuple-element.375), channel_id=1, source_target_pairs={{0,16},{16,32},{32,48},{48,64},{64,80},{80,96},{96,112},{112,128},... | collective-permute-start | bytes 196616 | tf_op jit(solution)/shard_map/while/body/eval_jaxpr/ppermute | solution.py:13
  164.5 8.3 %collective-permute-start = (bf16[256,128]{1,0:T(8,128)(2,1)S(1)}, bf16[256,128]{1,0:T(8,128)(2,1)S(1)}, u32[]{:S(2)}, u32[]{:S(2)}) collective-permute-start(bf16[256,128]{1,0:T(8,128)(2,1)S(1)} %get-tuple-element.374), channel_id=1, source_target_pairs={{0,16},{16,32},{32,48},{48,64},{64,80},{80,96},{96,112},{112,128},... | collective-permute-start | bytes 196616 | tf_op jit(solution)/shard_map/while/body/eval_jaxpr/ppermute | solution.py:13
  166.4 8.3 %collective-permute-start.1 = (bf16[256,128]{1,0:T(8,128)(2,1)S(1)}, bf16[256,128]{1,0:T(8,128)(2,1)S(1)}, u32[]{:S(2)}, u32[]{:S(2)}) collective-permute-start(bf16[256,128]{1,0:T(8,128)(2,1)S(1)} %get-tuple-element.375), channel_id=1, source_target_pairs={{0,16},{16,32},{32,48},{48,64},{64,80},{80,96},{96,112},{112,128},... | collective-permute-start | bytes 196616 | tf_op jit(solution)/shard_map/while/body/eval_jaxpr/ppermute | solution.py:13
  174.7 8.3 %collective-permute-start = (bf16[256,128]{1,0:T(8,128)(2,1)S(1)}, bf16[256,128]{1,0:T(8,128)(2,1)S(1)}, u32[]{:S(2)}, u32[]{:S(2)}) collective-permute-start(bf16[256,128]{1,0:T(8,128)(2,1)S(1)} %get-tuple-element.374), channel_id=1, source_target_pairs={{0,16},{16,32},{32,48},{48,64},{64,80},{80,96},{96,112},{112,128},... | collective-permute-start | bytes 196616 | tf_op jit(solution)/shard_map/while/body/eval_jaxpr/ppermute | solution.py:13
  176.6 8.3 %collective-permute-start.1 = (bf16[256,128]{1,0:T(8,128)(2,1)S(1)}, bf16[256,128]{1,0:T(8,128)(2,1)S(1)}, u32[]{:S(2)}, u32[]{:S(2)}) collective-permute-start(bf16[256,128]{1,0:T(8,128)(2,1)S(1)} %get-tuple-element.375), channel_id=1, source_target_pairs={{0,16},{16,32},{32,48},{48,64},{64,80},{80,96},{96,112},{112,128},... | collective-permute-start | bytes 196616 | tf_op jit(solution)/shard_map/while/body/eval_jaxpr/ppermute | solution.py:13
  210.1 139.5 %reduce-scatter.4.cloned.1.call-start = ((), (), s32[]{:S(2)}) async-start(), calls=%async_computation.5 | async-start | bytes 2785280
  225.2 6.7 %collective-permute-start.5 = (bf16[640,128]{1,0:T(8,128)(2,1)S(1)}, bf16[640,128]{1,0:T(8,128)(2,1)S(1)}, u32[]{:S(2)}, u32[]{:S(2)}) collective-permute-start(bf16[640,128]{1,0:T(8,128)(2,1)S(1)} %all_to_all.26), channel_id=1, source_target_pairs={{0,15},{1,0},{2,1},{3,2},{4,3},{5,4},{6,5},{7,6},{8,7},{9,8},{10,9... | collective-permute-start | bytes 491528 | tf_op jit(solution)/shard_map/ppermute | solution.py:119
  231.6 6.9 %collective-permute-start.6 = (bf16[640,128]{1,0:T(8,128)(2,1)S(1)}, bf16[640,128]{1,0:T(8,128)(2,1)S(1)}, u32[]{:S(2)}, u32[]{:S(2)}) collective-permute-start(bf16[640,128]{1,0:T(8,128)(2,1)S(1)} %collective-permute-done.4), channel_id=1, source_target_pairs={{0,1},{1,2},{2,3},{3,4},{4,5},{5,6},{6,7},{7,8},{8,9},{9,10},{10,1... | collective-permute-start | bytes 491528 | tf_op jit(solution)/shard_map/ppermute | solution.py:116
  231.9 6.7 %collective-permute-start.7 = (bf16[640,128]{1,0:T(8,128)(2,1)S(1)}, bf16[640,128]{1,0:T(8,128)(2,1)S(1)}, u32[]{:S(2)}, u32[]{:S(2)}) collective-permute-start(bf16[640,128]{1,0:T(8,128)(2,1)S(1)} %collective-permute-done.5), channel_id=1, source_target_pairs={{0,15},{1,0},{2,1},{3,2},{4,3},{5,4},{6,5},{7,6},{8,7},{9,8},{10,9... | collective-permute-start | bytes 491528 | tf_op jit(solution)/shard_map/ppermute | solution.py:119
  238.5 6.9 %collective-permute-start.8 = (bf16[640,128]{1,0:T(8,128)(2,1)S(1)}, bf16[640,128]{1,0:T(8,128)(2,1)S(1)}, u32[]{:S(2)}, u32[]{:S(2)}) collective-permute-start(bf16[640,128]{1,0:T(8,128)(2,1)S(1)} %collective-permute-done.6), channel_id=1, source_target_pairs={{0,1},{1,2},{2,3},{3,4},{4,5},{5,6},{6,7},{7,8},{8,9},{9,10},{10,1... | collective-permute-start | bytes 491528 | tf_op jit(solution)/shard_map/ppermute | solution.py:116
  238.5 6.9 %collective-permute-start.9 = (bf16[640,128]{1,0:T(8,128)(2,1)S(1)}, bf16[640,128]{1,0:T(8,128)(2,1)S(1)}, u32[]{:S(2)}, u32[]{:S(2)}) collective-permute-start(bf16[640,128]{1,0:T(8,128)(2,1)S(1)} %collective-permute-done.7), channel_id=1, source_target_pairs={{0,15},{1,0},{2,1},{3,2},{4,3},{5,4},{6,5},{7,6},{8,7},{9,8},{10,9... | collective-permute-start | bytes 491528 | tf_op jit(solution)/shard_map/ppermute | solution.py:119
  245.4 6.8 %collective-permute-start.10 = (bf16[640,128]{1,0:T(8,128)(2,1)S(1)}, bf16[640,128]{1,0:T(8,128)(2,1)S(1)}, u32[]{:S(2)}, u32[]{:S(2)}) collective-permute-start(bf16[640,128]{1,0:T(8,128)(2,1)S(1)} %collective-permute-done.8), channel_id=1, source_target_pairs={{0,1},{1,2},{2,3},{3,4},{4,5},{5,6},{6,7},{7,8},{8,9},{9,10},{10,1... | collective-permute-start | bytes 491528 | tf_op jit(solution)/shard_map/ppermute | solution.py:116
  245.4 6.8 %collective-permute-start.11 = (bf16[640,128]{1,0:T(8,128)(2,1)S(1)}, bf16[640,128]{1,0:T(8,128)(2,1)S(1)}, u32[]{:S(2)}, u32[]{:S(2)}) collective-permute-start(bf16[640,128]{1,0:T(8,128)(2,1)S(1)} %collective-permute-done.9), channel_id=1, source_target_pairs={{0,15},{1,0},{2,1},{3,2},{4,3},{5,4},{6,5},{7,6},{8,7},{9,8},{10,9... | collective-permute-start | bytes 491528 | tf_op jit(solution)/shard_map/ppermute | solution.py:119
  351.5 20.0 %all-to-all-start.2 = ((bf16[128,32,20]{0,2,1:T(8,128)(2,1)}), bf16[128,32,20]{0,2,1:T(8,128)(2,1)S(1)}, u32[]{:S(2)}, u32[]{:S(2)}) async-start(bf16[128,32,20]{0,2,1:T(8,128)(2,1)} %all_to_all.30), calls=%async_computation.2 | async-start | bytes 393216 | tf_op jit(solution)/shard_map/all_to_all | solution.py:144
  386.8 6.8 %collective-permute-start.2 = (bf16[256,128]{1,0:T(8,128)(2,1)S(1)}, bf16[256,128]{1,0:T(8,128)(2,1)S(1)}, u32[]{:S(2)}, u32[]{:S(2)}) collective-permute-start(bf16[256,128]{1,0:T(8,128)(2,1)S(1)} %get-tuple-element.397), channel_id=1, source_target_pairs={{16,0},{32,16},{48,32},{64,48},{80,64},{96,80},{112,96},{128,112},... | collective-permute-start | bytes 196616 | tf_op jit(solution)/shard_map/while/body/eval_jaxpr/ppermute | solution.py:13
  389.9 6.7 %collective-permute-start.3 = (bf16[256,128]{1,0:T(8,128)(2,1)S(1)}, bf16[256,128]{1,0:T(8,128)(2,1)S(1)}, u32[]{:S(2)}, u32[]{:S(2)}) collective-permute-start(bf16[256,128]{1,0:T(8,128)(2,1)S(1)} %get-tuple-element.398), channel_id=1, source_target_pairs={{16,0},{32,16},{48,32},{64,48},{80,64},{96,80},{112,96},{128,112},... | collective-permute-start | bytes 196616 | tf_op jit(solution)/shard_map/while/body/eval_jaxpr/ppermute | solution.py:13
  397.5 7.2 %collective-permute-start.2 = (bf16[256,128]{1,0:T(8,128)(2,1)S(1)}, bf16[256,128]{1,0:T(8,128)(2,1)S(1)}, u32[]{:S(2)}, u32[]{:S(2)}) collective-permute-start(bf16[256,128]{1,0:T(8,128)(2,1)S(1)} %get-tuple-element.397), channel_id=1, source_target_pairs={{16,0},{32,16},{48,32},{64,48},{80,64},{96,80},{112,96},{128,112},... | collective-permute-start | bytes 196616 | tf_op jit(solution)/shard_map/while/body/eval_jaxpr/ppermute | solution.py:13
  477.3 6.7 %collective-permute-start.2 = (bf16[256,128]{1,0:T(8,128)(2,1)S(1)}, bf16[256,128]{1,0:T(8,128)(2,1)S(1)}, u32[]{:S(2)}, u32[]{:S(2)}) collective-permute-start(bf16[256,128]{1,0:T(8,128)(2,1)S(1)} %get-tuple-element.397), channel_id=1, source_target_pairs={{16,0},{32,16},{48,32},{64,48},{80,64},{96,80},{112,96},{128,112},... | collective-permute-start | bytes 196616 | tf_op jit(solution)/shard_map/while/body/eval_jaxpr/ppermute | solution.py:13
  533.0 6.8 %collective-permute-start.2 = (bf16[256,128]{1,0:T(8,128)(2,1)S(1)}, bf16[256,128]{1,0:T(8,128)(2,1)S(1)}, u32[]{:S(2)}, u32[]{:S(2)}) collective-permute-start(bf16[256,128]{1,0:T(8,128)(2,1)S(1)} %get-tuple-element.397), channel_id=1, source_target_pairs={{16,0},{32,16},{48,32},{64,48},{80,64},{96,80},{112,96},{128,112},... | collective-permute-start | bytes 196616 | tf_op jit(solution)/shard_map/while/body/eval_jaxpr/ppermute | solution.py:13
  537.2 6.7 %collective-permute-start.3 = (bf16[256,128]{1,0:T(8,128)(2,1)S(1)}, bf16[256,128]{1,0:T(8,128)(2,1)S(1)}, u32[]{:S(2)}, u32[]{:S(2)}) collective-permute-start(bf16[256,128]{1,0:T(8,128)(2,1)S(1)} %get-tuple-element.398), channel_id=1, source_target_pairs={{16,0},{32,16},{48,32},{64,48},{80,64},{96,80},{112,96},{128,112},... | collective-permute-start | bytes 196616 | tf_op jit(solution)/shard_map/while/body/eval_jaxpr/ppermute | solution.py:13
  (46 other events, 535.7 us)
Sparse Core Ops, SparseCore 0:
  210.3 43.4 all-gather.1
  289.1 60.5 reduce-scatter.3
